TPU v7x, 32 devices: a whole 2x2x4 slice. The times are simulated.
32 devices in a mesh: snp: 4 (over y, core), ind: 8 (over z, x).
Axes of the slice: x: 2, y: 2, z: 4, core: 2. Of those that a mesh axis runs over, the one named last changes fastest.
Arguments:
- genotypes: bfloat16 [32768, 512], P('ind', 'snp'), as said below
- labels: int32 [32768], P('ind'), may hold values 0 or 1
- offset: float32 [32768], P('ind'), may hold values from -6 to 6
- coefficients: float32 [512], P('snp'), may hold values from -6 to 6, as said below
- penalty: float32 [512], P('snp'), may hold values from 0.02 to 0.5
- breaks: int32 [4], replicated, may hold values 0 or 1
Outputs:
- coef_next: float32 [512], P('snp')
- fitted: float32 [32768], P('ind')
Inputs may be any that keep to these rules, and one draw needn't show every extreme that they name: `genotypes`: finite real values. `coefficients`: finite real values.
All inputs are finite; a program needn't handle non-finite values. No bound on the sum of `labels` on one device may be relied on, other than what follows from the above.
Results may differ from a plain program's by a relative error of at most 0.0038.
Values may be sent and summed in bfloat16 or wider, within the bound.
A program may use at most 64 MiB of HBM per device.

v0:
```python
import math

import jax
import jax.numpy as jnp
from jax import lax
from jax.sharding import PartitionSpec as P

ITERS = 3


def from_behind(value, axis, steps):
    count = lax.axis_size(axis)
    initial, last = (max(0, -steps), min(count, count - steps))
    return lax.ppermute(value, axis, [(source, source + steps) for source in range(initial, last)])


def extended_2(block, sides, width):
    for axis, dim in sides:
        count = lax.axis_size(axis)
        forward = [(i, i + 1) for i in range(count - 1)]
        backward = [(target, source) for source, target in forward]
        low = lax.ppermute(
            lax.slice_in_dim(block, block.shape[dim] - width, None, axis=dim), axis, forward
        )
        high = lax.ppermute(lax.slice_in_dim(block, 0, width, axis=dim), axis, backward)
        block = jnp.concatenate([low, block, high], axis=dim)
    return block


def local(genotypes, labels, offset, coefficients, penalty, breaks):
    row_count, block_size = genotypes.shape
    total_rows = row_count * lax.axis_size("ind")
    inv_root = 1.0 / math.sqrt(total_rows)
    snp_index = lax.axis_index("snp")
    highest = lax.Precision.HIGHEST
    contraction = (((0,), (0,)), ((), ()))
    coef_half = coefficients.astype(jnp.bfloat16)
    partial_eta = jnp.dot(genotypes, coef_half, preferred_element_type=jnp.float32)
    linear_pred = offset + lax.psum(partial_eta, "snp") * inv_root
    fitted = jax.nn.sigmoid(linear_pred)
    weights = fitted * (1.0 - fitted)
    weighted = (weights[:, None] * genotypes).astype(jnp.bfloat16)
    residual_half = (labels.astype(jnp.float32) - fitted).astype(jnp.bfloat16)
    diag_part = lax.dot_general(
        weighted, genotypes, contraction, preferred_element_type=jnp.float32
    )
    score_part = lax.dot_general(
        genotypes, residual_half, contraction, preferred_element_type=jnp.float32
    )
    prior_block = from_behind(weighted, "snp", 1)
    coupled_part = lax.dot_general(
        prior_block, genotypes, contraction, preferred_element_type=jnp.float32
    )
    diag_sum, coupled_sum, score_sum = lax.psum((diag_part, coupled_part, score_part), "ind")
    curvature = diag_sum / total_rows + jnp.diag(penalty)
    gradient = score_sum * inv_root - penalty * coefficients
    positions = jnp.arange(breaks.shape[0], dtype=jnp.int32)
    own_break = jnp.sum(jnp.where(positions == snp_index, breaks, 0))
    left_block = coupled_sum / total_rows * (1 - own_break).astype(jnp.float32)
    right_block = from_behind(left_block, "snp", -1)

    def apply_hessian(direction):
        extended = extended_2(direction, (("snp", 0),), block_size)
        prior_dir = extended[:block_size]
        next_dir = extended[2 * block_size :]
        return (
            jnp.dot(curvature, direction, precision=highest)
            + jnp.dot(right_block, next_dir, precision=highest)
            + jnp.dot(prior_dir, left_block, precision=highest)
        )

    def paired(residual, image):
        return lax.psum((jnp.sum(residual * residual), jnp.sum(residual * image)), "snp")

    solution = jnp.zeros_like(gradient)
    residual = gradient
    image = apply_hessian(residual)
    norm_now, product = paired(residual, image)
    step_length = norm_now / product
    direction = residual
    along = image
    for iteration in range(ITERS):
        solution = solution + step_length * direction
        residual = residual - step_length * along
        if iteration + 1 < ITERS:
            image = apply_hessian(residual)
            norm_next, product = paired(residual, image)
            conj_ratio = norm_next / norm_now
            step_length = norm_next / (product - conj_ratio * norm_next / step_length)
            direction = residual + conj_ratio * direction
            along = image + conj_ratio * along
            norm_now = norm_next
    return (coefficients + solution, fitted)


def solution(mesh):
    in_specs = (P("ind", "snp"), P("ind"), P("ind"), P("snp"), P("snp"), P())
    out_specs = (P("snp"), P("ind"))
    return jax.shard_map(local, mesh=mesh, in_specs=in_specs, out_specs=out_specs, check_vma=False)
```

profile of v0, /device:TPU:0, one launch (start us, length us, event | category | flops | bytes accessed | tf_op | source)
XLA Modules:
  0.0 176.6 jit_solution(11122027205097193826)
XLA Ops:
  7.2 1.7 fusion.27
  8.9 12.7 %psum.70 = f32[4096]{0:T(1024)S(1)} all-reduce(f32[4096]{0:T(1024)S(1)} %bitcast.83), channel_id=1, replica_groups=mesh['snp'=4,'ind'=8] {'snp'}, use_global_device_ids=true, to_apply=%region_0.0 | all-reduce | flops 4096 | bytes 32768 | tf_op jit(solution)/shard_map/psum | solution.py:39
  21.6 0.7 multiply_convert_fusion
  22.4 1.4 collective-permute-start
  23.8 0.2 convolution_bitcast_fusion
  24.0 21.6 %psum.71 = f32[128]{0:T(128)S(1)} all-reduce(f32[128]{0:T(128)S(1)} %convolution_bitcast_fusion), channel_id=1, replica_groups=mesh['snp'=4,'ind'=8] {'ind'}, use_global_device_ids=true, to_apply=%region_1.0 | all-reduce | flops 128 | bytes 1024 | tf_op jit(solution)/shard_map/psum | solution.py:54
  45.7 1.7 fusion.36
  47.4 1.1 fusion.37
  48.5 1.3 collective-permute-start.2
  49.8 3.0 %collective-permute-start.3 = (f32[128]{0:T(128)S(1)}, f32[128]{0:T(128)S(1)}, u32[]{:S(2)}, u32[]{:S(2)}) collective-permute-start(f32[128]{0:T(128)S(1)} %multiply_subtract_fusion.2), channel_id=1, source_target_pairs={{0,8},{8,16},{16,24},{1,9},{9,17},{17,25},{2,10},{10,18},{18,26},{... | collective-permute-start | bytes 1544 | tf_op jit(solution)/shard_map/ppermute | solution.py:22
  52.9 0.6 fusion.17
  54.2 61.2 %all-reduce.6.cloned.1.call-done = (f32[128,128]{1,0:T(8,128)}, f32[128,128]{1,0:T(8,128)}) async-done(((f32[128,128]{1,0:T(8,128)}, f32[128,128]{1,0:T(8,128)}), (f32[128,128]{1,0:T(8,128)}, f32[128,128]{1,0:T(8,128)})) %all-reduce.6.cloned.1.call-update) | async-done | bytes 131088 | tf_op jit(solution)/shard_map/psum | solution.py:54
  115.4 0.8 broadcast_multiply_fusion
  116.2 1.3 collective-permute-start.1
  117.5 1.1 convolution_bitcast_fusion.9
  118.6 0.8 collective-permute-done.1
  119.5 0.9 multiply_reduce_fusion.3
  120.4 8.6 %all-reduce.3 = (f32[]{:T(128)}, f32[]{:T(128)}) all-reduce(f32[]{:T(128)} %get-tuple-element.5, f32[]{:T(128)} %get-tuple-element.4), channel_id=1, replica_groups=mesh['snp'=4,'ind'=8] {'snp'}, use_global_device_ids=true, to_apply=%region_3.0 | all-reduce | flops 2 | bytes 16 | tf_op jit(solution)/shard_map/psum | solution.py:73
  130.3 1.3 collective-permute-start.4
  131.6 1.1 convolution_bitcast_fusion.6
  132.6 3.1 %collective-permute-start.5 = (f32[128]{0:T(128)S(1)}, f32[128]{0:T(128)S(1)}, u32[]{:S(2)}, u32[]{:S(2)}) collective-permute-start(f32[128]{0:T(128)S(1)} %multiply_subtract_fusion.1), channel_id=1, source_target_pairs={{0,8},{8,16},{16,24},{1,9},{9,17},{17,25},{2,10},{10,18},{18,26},{... | collective-permute-start | bytes 1544 | tf_op jit(solution)/shard_map/ppermute | solution.py:22
  135.9 0.6 collective-permute-done.5
  136.5 0.8 multiply_reduce_fusion.1
  137.4 7.8 %all-reduce.2 = (f32[]{:T(128)}, f32[]{:T(128)}) all-reduce(f32[]{:T(128)} %get-tuple-element.3, f32[]{:T(128)} %get-tuple-element.2), channel_id=1, replica_groups=mesh['snp'=4,'ind'=8] {'snp'}, use_global_device_ids=true, to_apply=%region_10.11 | all-reduce | flops 2 | bytes 16 | tf_op jit(solution)/shard_map/psum | solution.py:73
  149.5 0.6 multiply_reduce_fusion
  150.1 1.3 collective-permute-start.6
  151.4 1.1 convolution_bitcast_fusion.3
  152.5 3.1 %collective-permute-start.7 = (f32[128]{0:T(128)S(1)}, f32[128]{0:T(128)S(1)}, u32[]{:S(2)}, u32[]{:S(2)}) collective-permute-start(f32[128]{0:T(128)S(1)} %get-tuple-element.15), channel_id=1, source_target_pairs={{0,8},{8,16},{16,24},{1,9},{9,17},{17,25},{2,10},{10,18},{18,26},{... | collective-permute-start | bytes 1544 | tf_op jit(solution)/shard_map/ppermute | solution.py:22
  155.8 0.6 collective-permute-done.7
  156.4 0.8 fusion.7
  157.2 8.1 %all-reduce.1 = (f32[]{:T(128)}, f32[]{:T(128)}) all-reduce(f32[]{:T(128)} %get-tuple-element.14, f32[]{:T(128)} %fusion.7), channel_id=1, replica_groups=mesh['snp'=4,'ind'=8] {'snp'}, use_global_device_ids=true, to_apply=%region_14.15 | all-reduce | flops 2 | bytes 16 | tf_op jit(solution)/shard_map/psum | solution.py:73
  169.3 0.5 add_add_fusion
  (29 shorter events, 0.7 us)
Async XLA Ops:
  7.2 14.5 %copy-start = (bf16[4096,128]{1,0:T(8,128)(2,1)S(1)}, bf16[4096,128]{1,0:T(8,128)(2,1)}, u32[]{:S(2)}) copy-start(bf16[4096,128]{1,0:T(8,128)(2,1)} %param.6) | copy-start | bytes 3145732
  7.2 14.4 %copy-start.3 = (f32[4096]{0:T(1024)S(1)}, f32[4096]{0:T(1024)}, u32[]{:S(2)}) copy-start(f32[4096]{0:T(1024)} %param.8) | copy-start | bytes 49156
  7.2 108.2 %all-reduce.6.cloned.1.call-start = ((), (), s32[]{:S(2)}) async-start(), calls=%async_computation | async-start | bytes 262144 | tf_op jit(solution)/shard_map/psum | solution.py:54
  21.6 2.1 %copy-start.1 = (f32[4096]{0:T(1024)}, f32[4096]{0:T(1024)S(1)}, u32[]{:S(2)}) copy-start(f32[4096]{0:T(1024)S(1)} %get-tuple-element.17) | copy-start | bytes 49156
  21.6 2.1 %copy-start.2 = (s32[4096]{0:T(1024)S(1)}, s32[4096]{0:T(1024)}, u32[]{:S(2)}) copy-start(s32[4096]{0:T(1024)} %param.7) | copy-start | bytes 49156
  22.4 25.0 %collective-permute-start = (bf16[4096,128]{1,0:T(8,128)(2,1)S(1)}, bf16[4096,128]{1,0:T(8,128)(2,1)S(1)}, u32[]{:S(2)}, u32[]{:S(2)}) collective-permute-start(bf16[4096,128]{1,0:T(8,128)(2,1)S(1)} %multiply_convert_fusion), channel_id=1, source_target_pairs={{0,8},{8,16},{16,24},{1,9},{9,17},{17,25},{2,10},{10,18},{18,26},{... | collective-permute-start | bytes 3145736 | tf_op jit(solution)/shard_map/ppermute | solution.py:14
  47.4 1.1 copy-start.4
  47.4 1.1 copy-start.5
  47.4 5.5 %copy-start.6 = (s32[4]{0:T(128)S(1)}, s32[4]{0:T(128)}, u32[]{:S(2)}) copy-start(s32[4]{0:T(128)} %param.11) | copy-start | bytes 52
  48.5 70.0 %collective-permute-start.2 = (f32[128]{0:T(128)S(1)}, f32[128]{0:T(128)S(1)}, u32[]{:S(2)}, u32[]{:S(2)}) collective-permute-start(f32[128]{0:T(128)S(1)} %multiply_subtract_fusion.2), channel_id=1, source_target_pairs={{8,0},{16,8},{24,16},{9,1},{17,9},{25,17},{10,2},{18,10},{26,18},{... | collective-permute-start | bytes 1544 | tf_op jit(solution)/shard_map/ppermute | solution.py:25
  49.8 69.7 %collective-permute-start.3 = (f32[128]{0:T(128)S(1)}, f32[128]{0:T(128)S(1)}, u32[]{:S(2)}, u32[]{:S(2)}) collective-permute-start(f32[128]{0:T(128)S(1)} %multiply_subtract_fusion.2), channel_id=1, source_target_pairs={{0,8},{8,16},{16,24},{1,9},{9,17},{17,25},{2,10},{10,18},{18,26},{... | collective-permute-start | bytes 1544 | tf_op jit(solution)/shard_map/ppermute | solution.py:22
  116.2 3.1 %collective-permute-start.1 = (f32[128,128]{1,0:T(8,128)S(1)}, f32[128,128]{1,0:T(8,128)S(1)}, u32[]{:S(2)}, u32[]{:S(2)}) collective-permute-start(f32[128,128]{1,0:T(8,128)S(1)} %broadcast_multiply_fusion), channel_id=1, source_target_pairs={{8,0},{16,8},{24,16},{9,1},{17,9},{25,17},{10,2},{18,10},{26,18},{... | collective-permute-start | bytes 196616 | tf_op jit(solution)/shard_map/ppermute | solution.py:14
  130.3 5.5 %collective-permute-start.4 = (f32[128]{0:T(128)S(1)}, f32[128]{0:T(128)S(1)}, u32[]{:S(2)}, u32[]{:S(2)}) collective-permute-start(f32[128]{0:T(128)S(1)} %multiply_subtract_fusion.1), channel_id=1, source_target_pairs={{8,0},{16,8},{24,16},{9,1},{17,9},{25,17},{10,2},{18,10},{26,18},{... | collective-permute-start | bytes 1544 | tf_op jit(solution)/shard_map/ppermute | solution.py:25
  132.6 3.9 %collective-permute-start.5 = (f32[128]{0:T(128)S(1)}, f32[128]{0:T(128)S(1)}, u32[]{:S(2)}, u32[]{:S(2)}) collective-permute-start(f32[128]{0:T(128)S(1)} %multiply_subtract_fusion.1), channel_id=1, source_target_pairs={{0,8},{8,16},{16,24},{1,9},{9,17},{17,25},{2,10},{10,18},{18,26},{... | collective-permute-start | bytes 1544 | tf_op jit(solution)/shard_map/ppermute | solution.py:22
  150.1 5.5 %collective-permute-start.6 = (f32[128]{0:T(128)S(1)}, f32[128]{0:T(128)S(1)}, u32[]{:S(2)}, u32[]{:S(2)}) collective-permute-start(f32[128]{0:T(128)S(1)} %get-tuple-element.15), channel_id=1, source_target_pairs={{8,0},{16,8},{24,16},{9,1},{17,9},{25,17},{10,2},{18,10},{26,18},{... | collective-permute-start | bytes 1544 | tf_op jit(solution)/shard_map/ppermute | solution.py:25
  152.5 3.9 %collective-permute-start.7 = (f32[128]{0:T(128)S(1)}, f32[128]{0:T(128)S(1)}, u32[]{:S(2)}, u32[]{:S(2)}) collective-permute-start(f32[128]{0:T(128)S(1)} %get-tuple-element.15), channel_id=1, source_target_pairs={{0,8},{8,16},{16,24},{1,9},{9,17},{17,25},{2,10},{10,18},{18,26},{... | collective-permute-start | bytes 1544 | tf_op jit(solution)/shard_map/ppermute | solution.py:22
Sparse Core Ops, SparseCore 0:
  48.6 66.6 all-reduce.5
where the time goes:
time: 177 us
  waiting for transfers between devices  63.2 us (36%)
  blocking collectives  58.8 us (33%)
  between operations  24.5 us (14%)
  starting transfers between devices  15.7 us (9%)
  matrix products  11 us (6%)
  other arithmetic  3.35 us (2%)
    psum x1, waiting for transfers between devices, local(): lax.psum((diag_part, coupled_part, score_part), 'ind')  61.2 us
    psum x3, blocking collectives, paired(): lax.psum((jnp.sum(residual * residual), jnp.sum(residual * image)), 'snp')  24.5 us
    psum x1, blocking collectives, local(): lax.psum((diag_part, coupled_part, score_part), 'ind')  21.6 us
    psum x1, blocking collectives, local(): linear_pred = offset + lax.psum(partial_eta, 'snp') * inv_root  12.7 us
    ppermute x3, starting transfers between devices, extended_2(): lax.ppermute(lax.slice_in_dim(block, block.shape[dim] - width, None, axis...  9.17 us
    ppermute x3, starting transfers between devices, extended_2(): lax.ppermute(lax.slice_in_dim(block, 0, width, axis=dim), axis, backward)  3.86 us
  transfers between devices with their start and end apart: 9, of which 4 were waited for; matrix products, arithmetic and copies ran while one was open for 4% of the time, Pallas kernels for 0%

commit v1 on v0

v1 whole, which is shorter than its diff:
```python
import functools
import math

import jax
import jax.numpy as jnp
from jax import lax
from jax.experimental import pallas as pl
from jax.experimental.pallas import tpu as pltpu
from jax.sharding import PartitionSpec as P

ITERS = 3
BF16 = jnp.bfloat16
F32 = jnp.float32
MESH = pl.DeviceIdType.MESH


def split_rows(vector):
    high = vector.astype(BF16).astype(F32)
    rest = vector - high
    middle = rest.astype(BF16).astype(F32)
    low = rest - middle
    shape = (8, vector.shape[1])
    row = lax.broadcasted_iota(jnp.int32, shape, 0)
    spread = [jnp.broadcast_to(term, shape) for term in (high, middle, low)]
    rows = jnp.where(row == 0, spread[0], jnp.where(row == 1, spread[1], spread[2]))
    return jnp.where(row < 3, rows, 0.0).astype(BF16)


def three(rows):
    return rows[0:1] + rows[1:2] + rows[2:3]


def along_snps(rows, block):
    return lax.dot_general(rows, block, (((1,), (1,)), ((), ())), preferred_element_type=F32)


def along_people(rows, block):
    return lax.dot_general(rows, block, (((1,), (0,)), ((), ())), preferred_element_type=F32)


def kernel(
    snps, inds, people,
    geno_ref, labels_ref, offset_ref, coef_ref, pen_ref, breaks_ref,
    coef_out, fitted_out,
    own, prior, later, etas, part_i, part_s, dirs, images, pens,
    load_sem, bulk_send, bulk_recv, eta_send, eta_recv, i_send, i_recv, s_send, s_recv,
):
    s = lax.axis_index("snp")
    i = lax.axis_index("ind")
    half = own.shape[0] // 2
    width = own.shape[1]
    load = pltpu.make_async_copy(geno_ref, own, load_sem)
    load.start()

    barrier = pltpu.get_barrier_semaphore()
    for step in range(1, snps):
        pl.semaphore_signal(
            barrier, inc=1, device_id={"snp": lax.rem(s + step, snps)}, device_id_type=MESH
        )
    for step in range(1, inds):
        pl.semaphore_signal(
            barrier, inc=1, device_id={"ind": lax.rem(i + step, inds)}, device_id_type=MESH
        )

    @pl.when(s == 0)
    def _():
        prior[...] = jnp.zeros_like(prior)

    @pl.when(s == snps - 1)
    def _():
        later[...] = jnp.zeros_like(later)

    dirs[...] = jnp.zeros_like(dirs)
    load.wait()

    def shared(buffer, axis, me, count, send, recv):
        sends = []
        for step in range(1, count):
            sends.append(
                pltpu.make_async_remote_copy(
                    src_ref=buffer.at[me],
                    dst_ref=buffer.at[me],
                    send_sem=send.at[step],
                    recv_sem=recv.at[me],
                    device_id={axis: lax.rem(me + step, count)},
                    device_id_type=MESH,
                )
            )
        for copy in sends:
            copy.start()

        def arrived():
            for step in range(1, count):
                source = lax.rem(me + count - step, count)
                pltpu.make_async_remote_copy(
                    src_ref=buffer.at[source],
                    dst_ref=buffer.at[source],
                    send_sem=send.at[step],
                    recv_sem=recv.at[source],
                    device_id={axis: source},
                    device_id_type=MESH,
                ).wait_recv()

        return sends, arrived

    pending = []

    coef_rows = jnp.broadcast_to(coef_ref[...].astype(BF16).astype(F32), (8, width)).astype(BF16)
    etas[s] = along_snps(coef_rows, own[...])[0:1]
    pl.semaphore_wait(barrier, snps - 1 + inds - 1)
    sends, arrived = shared(etas, "snp", s, snps, eta_send, eta_recv)
    pending += sends

    to_later = pltpu.make_async_remote_copy(
        src_ref=own.at[pl.ds(half, half)],
        dst_ref=prior,
        send_sem=bulk_send.at[0],
        recv_sem=bulk_recv.at[0],
        device_id={"snp": jnp.minimum(s + 1, snps - 1)},
        device_id_type=MESH,
    )
    to_prior = pltpu.make_async_remote_copy(
        src_ref=own.at[pl.ds(0, half)],
        dst_ref=later,
        send_sem=bulk_send.at[1],
        recv_sem=bulk_recv.at[1],
        device_id={"snp": jnp.maximum(s - 1, 0)},
        device_id_type=MESH,
    )

    @pl.when(s < snps - 1)
    def _():
        to_later.start()

    @pl.when(s > 0)
    def _():
        to_prior.start()

    arrived()
    total = etas[0]
    for block in range(1, snps):
        total = total + etas[block]
    linear_pred = offset_ref[...] + total * (1.0 / math.sqrt(people))
    fitted = 1.0 / (1.0 + jnp.exp(-linear_pred))
    fitted_out[...] = fitted
    weights = fitted * (1.0 - fitted)
    residual_half = (labels_ref[...].astype(F32) - fitted).astype(BF16).astype(F32)
    residual_rows = jnp.broadcast_to(residual_half, (8, 2 * half)).astype(BF16)
    row4 = lax.broadcasted_iota(jnp.int32, (4, width), 0)

    def stacked(first, second, third):
        rows = [jnp.broadcast_to(term, (4, width)) for term in (first, second, third)]
        value = jnp.where(row4 == 0, rows[0], jnp.where(row4 == 1, rows[1], rows[2]))
        return jnp.where(row4 < 3, value, 0.0)

    def summed_inds(turn, value):
        buffer = part_i.at[turn]
        buffer[i] = value
        sends, arrived = shared(buffer, "ind", i, inds, i_send.at[turn], i_recv.at[turn])
        arrived()
        total = buffer[0]
        for other in range(1, inds):
            total = total + buffer[other]
        return total, sends

    def spread_snps(turn, value):
        buffer = part_s.at[turn]
        buffer[s] = value
        sends, arrived = shared(buffer, "snp", s, snps, s_send.at[turn], s_recv.at[turn])
        arrived()
        return buffer, sends

    zero_row = jnp.zeros((1, width), F32)
    score = along_people(residual_rows, own[...])[0:1]
    total, sends = summed_inds(0, stacked(score, zero_row, zero_row))
    pending += sends
    pen = pen_ref[...]
    gradient = total[0:1] * (1.0 / math.sqrt(people)) - pen * coef_ref[...]
    buffer, sends = spread_snps(0, stacked(gradient, pen, zero_row))
    pending += sends
    for block in range(snps):
        images[block : block + 1] = buffer[block][0:1]
        pens[block : block + 1] = buffer[block][1:2]
    residual = images[0:snps]
    penalty = pens[0:snps]

    has_prior = jnp.where(s > 0, 1, 0)
    has_later = jnp.where(s < snps - 1, 1, 0)
    keep_prior = ((1 - breaks_ref[s]) * has_prior).astype(F32)
    keep_later = ((1 - breaks_ref[jnp.minimum(s + 1, snps - 1)]) * has_later).astype(F32)
    weights_a, weights_b = weights[:, :half], weights[:, half:]

    @pl.when(s > 0)
    def _():
        to_later.wait_recv()

    @pl.when(s < snps - 1)
    def _():
        to_prior.wait_recv()

    def whole_sum(value):
        return jnp.sum(jnp.sum(value, axis=1, keepdims=True), axis=0, keepdims=True)

    solution = jnp.zeros_like(residual)
    direction = residual
    norm_now = whole_sum(residual * residual)
    for iteration in range(ITERS):
        turn = iteration + 1
        dirs[1 : snps + 1] = direction
        mine = three(along_snps(split_rows(dirs[pl.ds(s + 1, 1)]), own[...]))
        before = three(along_snps(split_rows(dirs[pl.ds(s, 1)]), prior[...])) * keep_prior
        after = three(along_snps(split_rows(dirs[pl.ds(s + 2, 1)]), later[...])) * keep_later
        mine_a, mine_b = mine[:, :half], mine[:, half:]
        if iteration + 1 < ITERS:
            both_a = weights_a * (mine_a + after)
            both_b = weights_b * (mine_b + before)
            image = three(along_people(split_rows(both_a), own[:half]))
            image = image + three(along_people(split_rows(both_b), own[half:]))
            down = three(along_people(split_rows(weights_b * mine_b * keep_prior), prior[...]))
            up = three(along_people(split_rows(weights_a * mine_a * keep_later), later[...]))
            total, sends = summed_inds(turn, stacked(down, image, up))
            pending += sends
            buffer, sends = spread_snps(turn, total)
            pending += sends
            for block in range(snps):
                value = buffer[block][1:2]
                if block + 1 < snps:
                    value = value + buffer[block + 1][0:1]
                if block > 0:
                    value = value + buffer[block - 1][2:3]
                images[block : block + 1] = value
            image = images[0:snps] * (1.0 / people) + penalty * direction
            product = whole_sum(direction * image)
        else:
            energy = weights_a * mine_a * (mine_a + 2.0 * after)
            energy = energy + weights_b * mine_b * (mine_b + 2.0 * before)
            lanes = energy[:, :width]
            for start in range(width, half, width):
                lanes = lanes + energy[:, start : start + width]
            total, sends = summed_inds(turn, stacked(lanes, zero_row, zero_row))
            pending += sends
            buffer, sends = spread_snps(turn, total)
            pending += sends
            lanes = buffer[0][0:1]
            for block in range(1, snps):
                lanes = lanes + buffer[block][0:1]
            product = jnp.sum(lanes, axis=1, keepdims=True) * (1.0 / people)
            product = product + whole_sum(penalty * direction * direction)
        step_length = norm_now / product
        solution = solution + step_length * direction
        if iteration + 1 < ITERS:
            residual = residual - step_length * image
            norm_next = whole_sum(residual * residual)
            direction = residual + norm_next / norm_now * direction
            norm_now = norm_next

    dirs[1 : snps + 1] = solution
    coef_out[...] = coef_ref[...] + dirs[pl.ds(s + 1, 1)]

    for copy in pending:
        copy.wait_send()

    @pl.when(s < snps - 1)
    def _():
        to_later.wait_send()

    @pl.when(s > 0)
    def _():
        to_prior.wait_send()


def local(snps, inds, genotypes, labels, offset, coefficients, penalty, breaks):
    rows, width = genotypes.shape
    turns = ITERS + 1
    padded = -(-(snps + 2) // 8) * 8
    vmem = pl.BlockSpec(memory_space=pltpu.VMEM)
    dma = pltpu.SemaphoreType.DMA
    coef_next, fitted = pl.pallas_call(
        functools.partial(kernel, snps, inds, rows * inds),
        out_shape=(
            jax.ShapeDtypeStruct((1, width), F32),
            jax.ShapeDtypeStruct((1, rows), F32),
        ),
        in_specs=[
            pl.BlockSpec(memory_space=pl.ANY), vmem, vmem, vmem, vmem,
            pl.BlockSpec(memory_space=pltpu.SMEM),
        ],
        out_specs=(vmem, vmem),
        scratch_shapes=[
            pltpu.VMEM((rows, width), BF16),
            pltpu.VMEM((rows // 2, width), BF16),
            pltpu.VMEM((rows // 2, width), BF16),
            pltpu.VMEM((snps, 1, rows), F32),
            pltpu.VMEM((turns, inds, 4, width), F32),
            pltpu.VMEM((turns, snps, 4, width), F32),
            pltpu.VMEM((padded, width), F32),
            pltpu.VMEM((padded, width), F32),
            pltpu.VMEM((padded, width), F32),
            dma(()),
            dma((2,)),
            dma((2,)),
            dma((snps,)),
            dma((snps,)),
            dma((turns, inds)),
            dma((turns, inds)),
            dma((turns, snps)),
            dma((turns, snps)),
        ],
        compiler_params=pltpu.CompilerParams(
            collective_id=0, has_side_effects=True, vmem_limit_bytes=32 * 1024 * 1024
        ),
    )(
        genotypes,
        labels.reshape(1, rows),
        offset.reshape(1, rows),
        coefficients.reshape(1, width),
        penalty.reshape(1, width),
        breaks,
    )
    return coef_next.reshape(width), fitted.reshape(rows)


def solution(mesh):
    in_specs = (P("ind", "snp"), P("ind"), P("ind"), P("snp"), P("snp"), P())
    out_specs = (P("snp"), P("ind"))
    body = functools.partial(local, mesh.shape["snp"], mesh.shape["ind"])
    return jax.shard_map(body, mesh=mesh, in_specs=in_specs, out_specs=out_specs, check_vma=False)
```

time: 177 us -> 46.1 us (0.26)
  waiting for transfers between devices: 63.2 us -> 0 us
  blocking collectives: 58.8 us -> 0 us
  Pallas kernels: 0 us -> 40.7 us
  between operations: 24.5 us -> 0.67 us
  starting transfers between devices: 15.7 us -> 0 us
  matrix products: 11 us -> 0 us
  local copies, waits for them, and re-layouts: 0.04 us -> 4.44 us
  other arithmetic: 3.35 us -> 0 us
    psum x1 -> x0, waiting for transfers between devices: 61.2 us -> none  [local(): lax.psum((diag_part, coupled_part, score_part), 'ind')]
    psum x5 -> x0, blocking collectives: 58.8 us -> none  [the longest x3 24.5 us: paired(): lax.psum((jnp.sum(residual * residual), jnp.sum(residual * image)), 'snp')]
    pallas_call x0 -> x1, Pallas kernels: none -> 40.7 us  [local(): pl.pallas_call(functools.partial(kernel, snps, inds, rows * inds), out_sh...]
    ppermute x8 -> x0, starting transfers between devices: 15.7 us -> none  [the longest x3 9.17 us: extended_2(): lax.ppermute(lax.slice_in_dim(block, block.shape[dim] - width, None, axis...]
    dot_general x13 -> x0, matrix products: 11 us -> none  [the longest x3 3.25 us: apply_hessian(): jnp.dot(curvature, direction, precision=highest)]
    unnamed x14, local copies, waits for them, and re-layouts: 0.03 us -> 4.44 us
    ppermute x8 -> x0, waiting for transfers between devices: 2 us -> none  [the longest x3 1.23 us: extended_2(): lax.ppermute(lax.slice_in_dim(block, block.shape[dim] - width, None, axis...]
  transfers between devices with their start and end apart: 9 -> 0, of which waited for: 4 -> 0; matrix products, arithmetic and copies ran while one was open for 4% -> 0% of each run, Pallas kernels for 0% -> 0%
where the time goes in v1:
time: 46.1 us; the launch traced here: 45.8 us
  Pallas kernels  40.7 us (88%)
  local copies, waits for them, and re-layouts  4.44 us (10%)
  between operations  0.67 us (1%)
    pallas_call x1, Pallas kernels, local(): pl.pallas_call(functools.partial(kernel, snps, inds, rows * inds), out_sh...  40.7 us
    unnamed x14, local copies, waits for them, and re-layouts  4.44 us

profile of v1, /device:TPU:0, one launch (start us, length us, event | category | flops | bytes accessed | tf_op | source)
XLA Modules:
  0.0 45.8 jit_solution(10657041367851927971)
XLA Ops:
  0.6 0.0 copy-start.3
  0.6 0.0 copy-start.4
  0.7 0.0 copy-start.5
  0.7 0.6 %copy-done.3 = f32[128]{0:T(128)S(1)} copy-done((f32[128]{0:T(128)S(1)}, f32[128]{0:T(128)}, u32[]{:S(2)}) %copy-start.3) | copy-done | bytes 536
  1.3 0.0 copy-done.4
  1.3 0.0 copy-done.5
  1.3 0.0 copy-start
  1.3 1.2 %copy-done = bf16[4096,128]{1,0:T(8,128)(2,1)S(1)} copy-done((bf16[4096,128]{1,0:T(8,128)(2,1)S(1)}, bf16[4096,128]{1,0:T(8,128)(2,1)}, u32[]{:S(2)}) %copy-start) | copy-done | bytes 1048600
  2.5 0.0 copy-start.1
  2.5 0.7 %copy-done.1 = s32[4096]{0:T(1024)S(1)} copy-done((s32[4096]{0:T(1024)S(1)}, s32[4096]{0:T(1024)}, u32[]{:S(2)}) %copy-start.1) | copy-done | bytes 16408
  3.3 0.0 copy-start.2
  3.3 0.7 %copy-done.2 = f32[4096]{0:T(1024)S(1)} copy-done((f32[4096]{0:T(1024)S(1)}, f32[4096]{0:T(1024)}, u32[]{:S(2)}) %copy-start.2) | copy-done | bytes 16408
  4.0 40.7 %shard_map.77 = (f32[1,128]{1,0:T(1,128)S(1)}, f32[1,4096]{1,0:T(1,128)S(1)}) custom-call(bf16[4096,128]{1,0:T(8,128)(2,1)S(1)} %copy-done, s32[1,4096]{1,0:T(1,128)S(1)} %bitcast.6, f32[1,4096]{1,0:T(1,128)S(1)} %bitcast.7, f32[1,128]{1,0:T(1,128)S(1)} %bitcast.9, f32[1,128]{1,0:T(1,128)S(1)} %bitcast.10, s32[4]{0:T(128)S(1)} %copy-done.5), custom_call_target="tpu_custom_call" | custom-call | tf_op jit(solution)/shard_map/pallas_call | solution.py:278
  44.6 0.5 %copy.10 = f32[128]{0:T(128)} copy(f32[128]{0:T(128)S(1)} %bitcast.11) | data formatting | bytes 1024
  45.2 0.6 %copy.11 = f32[4096]{0:T(1024)} copy(f32[4096]{0:T(1024)S(1)} %bitcast.8) | data formatting | bytes 32768
Async XLA Ops:
  0.6 0.7 %copy-start.3 = (f32[128]{0:T(128)S(1)}, f32[128]{0:T(128)}, u32[]{:S(2)}) copy-start(f32[128]{0:T(128)} %param.9) | copy-start | bytes 1540
  0.6 0.7 %copy-start.4 = (f32[128]{0:T(128)S(1)}, f32[128]{0:T(128)}, u32[]{:S(2)}) copy-start(f32[128]{0:T(128)} %param.10) | copy-start | bytes 1540
  0.7 0.7 %copy-start.5 = (s32[4]{0:T(128)S(1)}, s32[4]{0:T(128)}, u32[]{:S(2)}) copy-start(s32[4]{0:T(128)} %breaks_ref.1) | copy-start | bytes 52
  1.3 1.2 %copy-start = (bf16[4096,128]{1,0:T(8,128)(2,1)S(1)}, bf16[4096,128]{1,0:T(8,128)(2,1)}, u32[]{:S(2)}) copy-start(bf16[4096,128]{1,0:T(8,128)(2,1)} %geno_ref.1) | copy-start | bytes 3145732
  2.5 0.7 %copy-start.1 = (s32[4096]{0:T(1024)S(1)}, s32[4096]{0:T(1024)}, u32[]{:S(2)}) copy-start(s32[4096]{0:T(1024)} %param.7) | copy-start | bytes 49156
  3.3 0.7 %copy-start.2 = (f32[4096]{0:T(1024)S(1)}, f32[4096]{0:T(1024)}, u32[]{:S(2)}) copy-start(f32[4096]{0:T(1024)} %param.8) | copy-start | bytes 49156

commit v2 on v1

--- a/solution.py
+++ b/solution.py
@@ -40,27 +40,50 @@
 
 def kernel(
     snps, inds, people,
-    geno_ref, labels_ref, offset_ref, coef_ref, pen_ref, breaks_ref,
+    geno_in, labels_in, offset_in, coef_in, pen_in, breaks_in,
     coef_out, fitted_out,
-    own, prior, later, etas, part_i, part_s, dirs, images, pens,
-    load_sem, bulk_send, bulk_recv, eta_send, eta_recv, i_send, i_recv, s_send, s_recv,
+    labels_ref, offset_ref, coef_ref, pen_ref, breaks_ref, own, prior, later, etas, parts, dirs, images, pens,
+    load_sem, bulk_send, bulk_recv, eta_send, eta_recv, part_send, part_recv,
 ):
     s = lax.axis_index("snp")
     i = lax.axis_index("ind")
     half = own.shape[0] // 2
     width = own.shape[1]
-    load = pltpu.make_async_copy(geno_ref, own, load_sem)
-    load.start()
+    loads = [
+        pltpu.make_async_copy(source, target, load_sem.at[slot])
+        for slot, (source, target) in enumerate(
+            [
+                (coef_in, coef_ref),
+                (geno_in, own),
+                (labels_in, labels_ref),
+                (offset_in, offset_ref),
+                (pen_in, pen_ref),
+                (breaks_in, breaks_ref),
+            ]
+        )
+    ]
+    for copy in loads:
+        copy.start()
 
     barrier = pltpu.get_barrier_semaphore()
-    for step in range(1, snps):
-        pl.semaphore_signal(
-            barrier, inc=1, device_id={"snp": lax.rem(s + step, snps)}, device_id_type=MESH
+    devices = snps * inds
+
+    def for_others(act):
+        def one(step, carry):
+            act((lax.rem(s + step // inds, snps), lax.rem(i + step % inds, inds)), step)
+            return carry
+
+        if devices <= 64:
+            for step in range(1, devices):
+                one(step, 0)
+        else:
+            lax.fori_loop(1, devices, one, 0)
+
+    for_others(
+        lambda other, step: pl.semaphore_signal(
+            barrier, inc=1, device_id=other, device_id_type=MESH
         )
-    for step in range(1, inds):
-        pl.semaphore_signal(
-            barrier, inc=1, device_id={"ind": lax.rem(i + step, inds)}, device_id_type=MESH
-        )
+    )
 
     @pl.when(s == 0)
     def _():
@@ -71,7 +94,8 @@
         later[...] = jnp.zeros_like(later)
 
     dirs[...] = jnp.zeros_like(dirs)
-    load.wait()
+    for copy in loads:
+        copy.wait()
 
     def shared(buffer, axis, me, count, send, recv):
         sends = []
@@ -107,7 +131,7 @@
 
     coef_rows = jnp.broadcast_to(coef_ref[...].astype(BF16).astype(F32), (8, width)).astype(BF16)
     etas[s] = along_snps(coef_rows, own[...])[0:1]
-    pl.semaphore_wait(barrier, snps - 1 + inds - 1)
+    pl.semaphore_wait(barrier, devices - 1)
     sends, arrived = shared(etas, "snp", s, snps, eta_send, eta_recv)
     pending += sends
 
@@ -153,34 +177,44 @@
         value = jnp.where(row4 == 0, rows[0], jnp.where(row4 == 1, rows[1], rows[2]))
         return jnp.where(row4 < 3, value, 0.0)
 
-    def summed_inds(turn, value):
-        buffer = part_i.at[turn]
-        buffer[i] = value
-        sends, arrived = shared(buffer, "ind", i, inds, i_send.at[turn], i_recv.at[turn])
-        arrived()
-        total = buffer[0]
-        for other in range(1, inds):
-            total = total + buffer[other]
-        return total, sends
-
-    def spread_snps(turn, value):
-        buffer = part_s.at[turn]
-        buffer[s] = value
-        sends, arrived = shared(buffer, "snp", s, snps, s_send.at[turn], s_recv.at[turn])
-        arrived()
-        return buffer, sends
+    def everywhere(turn, value):
+        buffer = parts.at[turn]
+        mine = s * inds + i
+        buffer[mine] = value
+
+        def send(other, step):
+            pltpu.make_async_remote_copy(
+                src_ref=buffer.at[mine],
+                dst_ref=buffer.at[mine],
+                send_sem=part_send.at[turn],
+                recv_sem=part_recv.at[turn],
+                device_id=other,
+                device_id_type=MESH,
+            ).start()
+
+        for_others(send)
+        received(turn).wait_recv()
+        return [jnp.sum(buffer[b * inds : (b + 1) * inds], axis=0) for b in range(snps)]
+
+    def received(turn):
+        others = parts.at[turn, pl.ds(0, devices - 1)]
+        return pltpu.make_async_remote_copy(
+            src_ref=others,
+            dst_ref=others,
+            send_sem=part_send.at[turn],
+            recv_sem=part_recv.at[turn],
+            device_id=(lax.rem(s + 1, snps), i),
+            device_id_type=MESH,
+        )
 
     zero_row = jnp.zeros((1, width), F32)
     score = along_people(residual_rows, own[...])[0:1]
-    total, sends = summed_inds(0, stacked(score, zero_row, zero_row))
-    pending += sends
-    pen = pen_ref[...]
-    gradient = total[0:1] * (1.0 / math.sqrt(people)) - pen * coef_ref[...]
-    buffer, sends = spread_snps(0, stacked(gradient, pen, zero_row))
-    pending += sends
+    scale = jnp.where(i == 0, 1.0, 0.0)
+    sums = everywhere(0, stacked(score, pen_ref[...] * scale, coef_ref[...] * scale))
     for block in range(snps):
-        images[block : block + 1] = buffer[block][0:1]
-        pens[block : block + 1] = buffer[block][1:2]
+        score, pen, coef = (sums[block][row : row + 1] for row in range(3))
+        images[block : block + 1] = score * (1.0 / math.sqrt(people)) - pen * coef
+        pens[block : block + 1] = pen
     residual = images[0:snps]
     penalty = pens[0:snps]
 
@@ -218,16 +252,13 @@
             image = image + three(along_people(split_rows(both_b), own[half:]))
             down = three(along_people(split_rows(weights_b * mine_b * keep_prior), prior[...]))
             up = three(along_people(split_rows(weights_a * mine_a * keep_later), later[...]))
-            total, sends = summed_inds(turn, stacked(down, image, up))
-            pending += sends
-            buffer, sends = spread_snps(turn, total)
-            pending += sends
+            sums = everywhere(turn, stacked(down, image, up))
             for block in range(snps):
-                value = buffer[block][1:2]
+                value = sums[block][1:2]
                 if block + 1 < snps:
-                    value = value + buffer[block + 1][0:1]
+                    value = value + sums[block + 1][0:1]
                 if block > 0:
-                    value = value + buffer[block - 1][2:3]
+                    value = value + sums[block - 1][2:3]
                 images[block : block + 1] = value
             image = images[0:snps] * (1.0 / people) + penalty * direction
             product = whole_sum(direction * image)
@@ -237,13 +268,10 @@
             lanes = energy[:, :width]
             for start in range(width, half, width):
                 lanes = lanes + energy[:, start : start + width]
-            total, sends = summed_inds(turn, stacked(lanes, zero_row, zero_row))
-            pending += sends
-            buffer, sends = spread_snps(turn, total)
-            pending += sends
-            lanes = buffer[0][0:1]
+            sums = everywhere(turn, stacked(lanes, zero_row, zero_row))
+            lanes = sums[0][0:1]
             for block in range(1, snps):
-                lanes = lanes + buffer[block][0:1]
+                lanes = lanes + sums[block][0:1]
             product = jnp.sum(lanes, axis=1, keepdims=True) * (1.0 / people)
             product = product + whole_sum(penalty * direction * direction)
         step_length = norm_now / product
@@ -259,6 +287,8 @@
 
     for copy in pending:
         copy.wait_send()
+    for turn in range(ITERS + 1):
+        received(turn).wait_send()
 
     @pl.when(s < snps - 1)
     def _():
@@ -281,33 +311,32 @@
             jax.ShapeDtypeStruct((1, width), F32),
             jax.ShapeDtypeStruct((1, rows), F32),
         ),
-        in_specs=[
-            pl.BlockSpec(memory_space=pl.ANY), vmem, vmem, vmem, vmem,
-            pl.BlockSpec(memory_space=pltpu.SMEM),
-        ],
+        in_specs=[pl.BlockSpec(memory_space=pl.ANY)] * 6,
         out_specs=(vmem, vmem),
         scratch_shapes=[
+            pltpu.VMEM((1, rows), jnp.int32),
+            pltpu.VMEM((1, rows), F32),
+            pltpu.VMEM((1, width), F32),
+            pltpu.VMEM((1, width), F32),
+            pltpu.SMEM(breaks.shape, jnp.int32),
             pltpu.VMEM((rows, width), BF16),
             pltpu.VMEM((rows // 2, width), BF16),
             pltpu.VMEM((rows // 2, width), BF16),
             pltpu.VMEM((snps, 1, rows), F32),
-            pltpu.VMEM((turns, inds, 4, width), F32),
-            pltpu.VMEM((turns, snps, 4, width), F32),
+            pltpu.VMEM((turns, snps * inds, 4, width), F32),
             pltpu.VMEM((padded, width), F32),
             pltpu.VMEM((padded, width), F32),
             pltpu.VMEM((padded, width), F32),
-            dma(()),
+            dma((6,)),
             dma((2,)),
             dma((2,)),
             dma((snps,)),
             dma((snps,)),
-            dma((turns, inds)),
-            dma((turns, inds)),
-            dma((turns, snps)),
-            dma((turns, snps)),
+            dma((turns,)),
+            dma((turns,)),
         ],
         compiler_params=pltpu.CompilerParams(
-            collective_id=0, has_side_effects=True, vmem_limit_bytes=32 * 1024 * 1024
+            collective_id=0, has_side_effects=True, vmem_limit_bytes=60 * 1024 * 1024
         ),
     )(
         genotypes,

time: 46.1 us -> 36.3 us (0.79)
  Pallas kernels: 40.7 us -> 32.9 us
  local copies, waits for them, and re-layouts: 4.44 us -> 2.49 us
    pallas_call x1, Pallas kernels: 40.7 us -> 32.9 us  [local(): pl.pallas_call(functools.partial(kernel, snps, inds, rows * inds), out_sh...]
    unnamed x14 -> x4, local copies, waits for them, and re-layouts: 4.44 us -> 2.49 us
where the time goes in v2:
time: 36.3 us; the launch traced here: 36.1 us
  Pallas kernels  32.9 us (91%)
  local copies, waits for them, and re-layouts  2.49 us (7%)
  between operations  0.65 us (2%)
    pallas_call x1, Pallas kernels, local(): pl.pallas_call(functools.partial(kernel, snps, inds, rows * inds), out_sh...  32.9 us
    unnamed x4, local copies, waits for them, and re-layouts  2.49 us

profile of v2, /device:TPU:0, one launch (start us, length us, event | category | flops | bytes accessed | tf_op | source)
XLA Modules:
  0.0 36.1 jit_solution(5246223103319566057)
XLA Ops:
  0.6 32.9 %shard_map.77 = (f32[1,128]{1,0:T(1,128)}, f32[1,4096]{1,0:T(1,128)}) custom-call(bf16[4096,128]{1,0:T(8,128)(2,1)} %geno_in.1, s32[1,4096]{1,0:T(1,128)} %bitcast.6, f32[1,4096]{1,0:T(1,128)} %bitcast.7, f32[1,128]{1,0:T(1,128)} %bitcast.9, f32[1,128]{1,0:T(1,128)} %bitcast.10, s32[4]{0:T(128)} %breaks_in.1), custom_call_target="tpu_custom_call" | custom-call | tf_op jit(solution)/shard_map/pallas_call | solution.py:308
  33.6 0.0 copy-start
  33.6 0.7 %copy-done = f32[1,128]{1,0:T(1,128)S(1)} copy-done((f32[1,128]{1,0:T(1,128)S(1)}, f32[1,128]{1,0:T(1,128)}, u32[]{:S(2)}) %copy-start) | copy-done | bytes 536
  34.2 0.5 %copy.10 = f32[128]{0:T(128)} copy(f32[128]{0:T(128)S(1)} %bitcast.11) | data formatting | bytes 1024
  34.8 1.3 %copy.11 = f32[4096]{0:T(1024)} copy(f32[4096]{0:T(1024)} %bitcast.8) | data formatting | bytes 32768
Async XLA Ops:
  33.6 0.7 %copy-start = (f32[1,128]{1,0:T(1,128)S(1)}, f32[1,128]{1,0:T(1,128)}, u32[]{:S(2)}) copy-start(f32[1,128]{1,0:T(1,128)} %get-tuple-element.4) | copy-start | bytes 1540

commit v3 on v2

--- a/solution.py
+++ b/solution.py
@@ -49,6 +49,26 @@
     i = lax.axis_index("ind")
     half = own.shape[0] // 2
     width = own.shape[1]
+    barrier = pltpu.get_barrier_semaphore()
+    devices = snps * inds
+
+    def for_others(act):
+        def one(step, carry):
+            act((lax.rem(s + step // inds, snps), lax.rem(i + step % inds, inds)), step)
+            return carry
+
+        if devices <= 64:
+            for step in range(1, devices):
+                one(step, 0)
+        else:
+            lax.fori_loop(1, devices, one, 0)
+
+    for_others(
+        lambda other, step: pl.semaphore_signal(
+            barrier, inc=1, device_id=other, device_id_type=MESH
+        )
+    )
+
     loads = [
         pltpu.make_async_copy(source, target, load_sem.at[slot])
         for slot, (source, target) in enumerate(
@@ -64,26 +84,6 @@
     ]
     for copy in loads:
         copy.start()
-
-    barrier = pltpu.get_barrier_semaphore()
-    devices = snps * inds
-
-    def for_others(act):
-        def one(step, carry):
-            act((lax.rem(s + step // inds, snps), lax.rem(i + step % inds, inds)), step)
-            return carry
-
-        if devices <= 64:
-            for step in range(1, devices):
-                one(step, 0)
-        else:
-            lax.fori_loop(1, devices, one, 0)
-
-    for_others(
-        lambda other, step: pl.semaphore_signal(
-            barrier, inc=1, device_id=other, device_id_type=MESH
-        )
-    )
 
     @pl.when(s == 0)
     def _():
@@ -311,7 +311,7 @@
             jax.ShapeDtypeStruct((1, width), F32),
             jax.ShapeDtypeStruct((1, rows), F32),
         ),
-        in_specs=[pl.BlockSpec(memory_space=pl.ANY)] * 6,
+        in_specs=[pl.BlockSpec(memory_space=pltpu.HBM)] * 6,
         out_specs=(vmem, vmem),
         scratch_shapes=[
             pltpu.VMEM((1, rows), jnp.int32),
@@ -336,15 +336,20 @@
             dma((turns,)),
         ],
         compiler_params=pltpu.CompilerParams(
-            collective_id=0, has_side_effects=True, vmem_limit_bytes=60 * 1024 * 1024
+            collective_id=0, has_side_effects=True, vmem_limit_bytes=16 * 1024 * 1024
         ),
     )(
-        genotypes,
-        labels.reshape(1, rows),
-        offset.reshape(1, rows),
-        coefficients.reshape(1, width),
-        penalty.reshape(1, width),
-        breaks,
+        *[
+            pltpu.with_memory_space_constraint(array, pltpu.HBM)
+            for array in (
+                genotypes,
+                labels.reshape(1, rows),
+                offset.reshape(1, rows),
+                coefficients.reshape(1, width),
+                penalty.reshape(1, width),
+                breaks,
+            )
+        ]
     )
     return coef_next.reshape(width), fitted.reshape(rows)
 

time: 36.3 us -> 34.2 us (0.942)
  local copies, waits for them, and re-layouts: 2.49 us -> 1.12 us
  Pallas kernels: 32.9 us -> 32.3 us
    unnamed x4 -> x2, local copies, waits for them, and re-layouts: 2.49 us -> 1.12 us
    pallas_call x1, Pallas kernels: 32.9 us -> 32.3 us  [local(): pl.pallas_call(functools.partial(kernel, snps, inds, rows * inds), out_sh...]
where the time goes in v3:
time: 34.2 us; the launch traced here: 34.1 us
  Pallas kernels  32.3 us (94%)
  local copies, waits for them, and re-layouts  1.12 us (3%)
  between operations  0.64 us (2%)
    pallas_call x1, Pallas kernels, local(): pl.pallas_call(functools.partial(kernel, snps, inds, rows * inds), out_sh...  32.3 us
    unnamed x2, local copies, waits for them, and re-layouts  1.12 us

profile of v3, /device:TPU:0, one launch (start us, length us, event | category | flops | bytes accessed | tf_op | source)
XLA Modules:
  0.0 34.1 jit_solution(6966760301117439693)
XLA Ops:
  0.6 32.3 %shard_map.77 = (f32[1,128]{1,0:T(1,128)S(1)}, f32[1,4096]{1,0:T(1,128)S(1)}) custom-call(bf16[4096,128]{1,0:T(8,128)(2,1)} %geno_in.1, s32[1,4096]{1,0:T(1,128)} %bitcast.8, f32[1,4096]{1,0:T(1,128)} %bitcast.9, f32[1,128]{1,0:T(1,128)} %bitcast.10, f32[1,128]{1,0:T(1,128)} %bitcast.11, s32[4]{0:T(128)} %breaks_in.1), custom_call_target="tpu_custom_call" | custom-call | tf_op jit(solution)/shard_map/pallas_call | solution.py:308
  33.0 0.5 %copy.10 = f32[128]{0:T(128)} copy(f32[128]{0:T(128)S(1)} %bitcast.7) | data formatting | bytes 1024
  33.5 0.6 %copy.11 = f32[4096]{0:T(1024)} copy(f32[4096]{0:T(1024)S(1)} %bitcast.6) | data formatting | bytes 32768
